TPU v7x, 128 devices: a whole 4x4x4 slice. The times are simulated.
128 devices in a mesh: row: 16 (over x, y), col: 8 (over z, core).
Axes of the slice: x: 4, y: 4, z: 4, core: 2. Of those that a mesh axis runs over, the one named last changes fastest.
Arguments:
- raw_rows: bfloat16 [131072, 64], P(('row', 'col')), may hold values from -6 to 6
- raw_wide: int32 [131072], P(('row', 'col')), may hold values from 0 to 1
- raw_dest: int32 [131072], P(('row', 'col')), may hold values from 0 to 127, as said below
- raw_slot: int32 [131072], P(('row', 'col')), may hold values from 0 to 511
- proj_narrow: bfloat16 [32, 128], replicated, may hold values from -1 to 1
- proj_wide: bfloat16 [64, 128], replicated, may hold values from -0.75 to 0.75
- adj_values: bfloat16 [32768, 32768], P('row', 'col'), may hold values from -1 to 1
- tile_mask: int32 [256, 256], P('row', 'col'), may hold values 0 or 1
- tile_scale: float32 [256, 256], P('row', 'col'), may hold values from 0.0041432036 to 0.041432038
- weight_sum: bfloat16 [2, 128, 128], replicated, may hold values from -0.5 to 0.5
- weight_product: bfloat16 [2, 128, 128], replicated, may hold values from -0.5 to 0.5
Outputs:
- user_out: bfloat16 [32768, 128], P(('row', 'col'))
- item_out: bfloat16 [8, 4096, 128], P('col', 'row')
Inputs may be any that keep to these rules, and one draw needn't show every extreme that they name: `raw_dest`: among the feature rows stored on one device at most 24 have any one destination; one device, drawn from the seed, is the destination of exactly 24 rows of every device.
All inputs are finite; a program needn't handle non-finite values. No bound on the sum of `tile_mask` on one device may be relied on, other than what follows from the above.
Results may differ from a plain program's by a relative error of at most 0.025.
Values may be sent and summed in bfloat16 or wider, within the bound.
A program may use at most 128 MiB of HBM per device.

v0:
```python
import jax
import jax.numpy as jnp
from jax import lax
from jax.sharding import PartitionSpec as P

D = 128
RAW_COLS = 64
NARROW = 32
TILE = 128
LAYERS = 2
UPD = 256
IPD = 256


def dequantize(values_bf, mask_tiles, scale_tiles):
    row_count = values_bf.shape[0]
    columns = values_bf.shape[1]
    values = values_bf.astype(jnp.float32)
    factor = mask_tiles.astype(jnp.float32) * scale_tiles
    tiled = (
        values.reshape(row_count // TILE, TILE, columns // TILE, TILE) * factor[:, None, :, None]
    )
    return tiled.reshape(row_count, columns).astype(jnp.bfloat16)


def update(side_sum, own_rows, weight_sum, weight_product):
    own_float = own_rows.astype(jnp.float32)
    summed = (side_sum + own_float).astype(jnp.bfloat16)
    product = (side_sum * own_float).astype(jnp.bfloat16)
    linear = jnp.dot(summed, weight_sum, preferred_element_type=jnp.float32)
    linear = linear + jnp.dot(product, weight_product, preferred_element_type=jnp.float32)
    return jnp.where(linear > 0, linear, 0.2 * linear).astype(jnp.bfloat16)


def per_device(
    raw_rows,
    raw_wide,
    raw_dest,
    raw_slot,
    proj_narrow,
    proj_wide,
    adj_values,
    tile_mask,
    tile_scale,
    weight_sum,
    weight_product,
):
    row_size = lax.axis_size("row")
    col_size = lax.axis_size("col")
    devices = row_size * col_size
    capacity = 3 * raw_rows.shape[0] // devices
    node_count = UPD + IPD
    targets = jnp.arange(devices, dtype=jnp.int32)
    onehot = (raw_dest[:, None] == targets[None, :]).astype(jnp.int32)
    rank_in_pair = jnp.sum((jnp.cumsum(onehot, axis=0) - onehot) * onehot, axis=1)
    position = raw_dest * capacity + rank_in_pair
    send_rows = jnp.zeros((devices * capacity, RAW_COLS), jnp.bfloat16).at[position].set(raw_rows)
    send_rows = send_rows.reshape(devices, capacity, RAW_COLS)
    send_codes = (
        jnp.full((devices * capacity,), -1, jnp.int32).at[position].set(raw_slot * 2 + raw_wide)
    )
    send_codes = send_codes.reshape(devices, capacity)
    rows_in = lax.all_to_all(send_rows, ("row", "col"), split_axis=0, concat_axis=0, tiled=True)
    codes_in = lax.all_to_all(send_codes, ("row", "col"), split_axis=0, concat_axis=0, tiled=True)
    wide_part = jnp.einsum("psc,cd->psd", rows_in, proj_wide, preferred_element_type=jnp.float32)
    narrow_part = jnp.einsum(
        "psc,cd->psd", rows_in[:, :, :NARROW], proj_narrow, preferred_element_type=jnp.float32
    )
    chosen = jnp.where((codes_in % 2 == 1)[:, :, None], wide_part, narrow_part)
    flat_codes = codes_in.reshape(-1)
    segment = jnp.where(flat_codes >= 0, flat_codes // 2, node_count).astype(jnp.int32)
    initial = jax.ops.segment_sum(chosen.reshape(-1, D), segment, num_segments=node_count + 1)
    initial = initial[:node_count].astype(jnp.bfloat16)
    user_rows = initial[:UPD]
    item_rows = initial[UPD:]
    adjacency = dequantize(adj_values, tile_mask, tile_scale)
    for layer_index in range(LAYERS):
        user_part = jnp.dot(
            adjacency,
            lax.all_gather(item_rows, "row", axis=0, tiled=True),
            preferred_element_type=jnp.float32,
        )
        item_part = lax.dot_general(
            adjacency,
            lax.all_gather(user_rows, "col", axis=0, tiled=True),
            (((0,), (0,)), ((), ())),
            preferred_element_type=jnp.float32,
        )
        user_side = lax.psum_scatter(
            user_part.astype(jnp.bfloat16), "col", scatter_dimension=0, tiled=True
        ).astype(jnp.float32)
        item_side = lax.psum_scatter(
            item_part.astype(jnp.bfloat16), "row", scatter_dimension=0, tiled=True
        ).astype(jnp.float32)
        new_users = update(
            user_side, user_rows, weight_sum[layer_index], weight_product[layer_index]
        )
        new_items = update(
            item_side, item_rows, weight_sum[layer_index], weight_product[layer_index]
        )
        user_rows = new_users
        item_rows = new_items
    return (user_rows, item_rows[None])


def solution(mesh):
    placed = (
        P(("row", "col"), None),
        P(("row", "col")),
        P(("row", "col")),
        P(("row", "col")),
        P(),
        P(),
        P("row", "col"),
        P("row", "col"),
        P("row", "col"),
        P(),
        P(),
    )
    return jax.shard_map(
        per_device,
        mesh=mesh,
        in_specs=placed,
        out_specs=(P(("row", "col"), None), P("col", "row", None)),
        check_vma=False,
    )
```

profile of v0, /device:TPU:0, one launch (start us, length us, event | category | flops | bytes accessed | tf_op | source)
XLA Modules:
  0.0 393.4 jit_solution(6186443028379261932)
XLA Ops:
  8.4 1.0 fusion.2
  10.2 4.3 %scatter_custom_fusion = s32[3072]{0:T(1024)S(1)} fusion(s32[1024]{0:T(1024)S(1)} %get-tuple-element.4, s32[1024]{0:T(1024)S(1)} %get-tuple-element.5, s32[]{:T(128)} %constant.40.clone.1), kind=kCustom, calls=%fused_computation.88 | custom fusion | bytes 12292 | tf_op jit(solution)/shard_map/scatter | solution.py:60
  15.2 11.1 %all-to-all-start = ((s32[128,1,24]{2,1,0:T(1,128)}), s32[128,1,24]{2,1,0:T(1,128)S(1)}, u32[]{:S(2)}, u32[]{:S(2)}) async-start(s32[128,1,24]{2,1,0:T(1,128)} %bitcast.4), calls=%async_computation | async-start | bytes 131072 | tf_op jit(solution)/shard_map/all_to_all | solution.py:64
  27.1 1.1 copy.23
  28.2 3.4 scatter_custom_fusion.1
  31.6 1.2 reshape.189
  32.8 3.0 all-to-all-done
  35.8 6.8 %all-to-all-start.1 = ((bf16[128,2,768]{2,1,0:T(2,128)(2,1)}), bf16[128,2,768]{2,1,0:T(2,128)(2,1)S(1)}, u32[]{:S(2)}, u32[]{:S(2)}) async-start(bf16[128,2,768]{2,1,0:T(2,128)(2,1)} %reshape.189), calls=%async_computation.1 | async-start | bytes 786432 | tf_op jit(solution)/shard_map/all_to_all | solution.py:63
  44.3 10.7 %all-to-all-done.1 = bf16[128,2,768]{2,1,0:T(2,128)(2,1)S(1)} async-done(((bf16[128,2,768]{2,1,0:T(2,128)(2,1)}), bf16[128,2,768]{2,1,0:T(2,128)(2,1)S(1)}, u32[]{:S(2)}, u32[]{:S(2)}) %all-to-all-start.1) | async-done | bytes 393248 | tf_op jit(solution)/shard_map/all_to_all | solution.py:63
  56.3 1.4 convolution_select_fusion
  58.7 17.3 %scatter_custom_fusion.2 = f32[513,128]{1,0:T(8,128)S(1)} fusion(s32[3072]{0:T(1024)S(1)} %bitcast.64, f32[3072,128]{1,0:T(8,128)S(1)} %bitcast.61, f32[]{:T(128)} %constant.23.clone.1), kind=kCustom, calls=%fused_computation.43 | custom fusion | flops 393216 | bytes 262660 | tf_op jit(solution)/shard_map/scatter-add | solution.py:72
  76.9 4.9 %mul.54 = f32[16,128,32,128]{3,2,1,0:T(8,128)S(1)} broadcast(f32[16,32]{1,0:T(8,128)S(1)} %convert_multiply_fusion.4), dimensions={0,2} | broadcast | bytes 33556480 | tf_op jit(solution)/shard_map/mul | solution.py:21
  81.8 26.4 %fusion = bf16[2048,4096]{1,0:T(8,128)(2,1)} fusion(f32[256,8,32,128]{3,2,1,0:T(8,128)S(1)} %bitcast.59, bf16[2048,4096]{1,0:T(8,128)(2,1)} %param.17), kind=kLoop, calls=%fused_computation.4 | loop fusion | flops 25165824 | bytes 67108864 | tf_op jit(solution)/shard_map/convert_element_type | solution.py:23
  108.2 13.1 %all_gather.12 = bf16[2048,128]{1,0:T(8,128)(2,1)S(1)} all-gather(bf16[256,128]{1,0:T(8,128)(2,1)S(1)} %get-tuple-element.2), channel_id=1, replica_groups=mesh['row'=16,'col'=8] {'col'}, dimensions={0}, use_global_device_ids=true | all-gather | bytes 589824 | tf_op jit(solution)/shard_map/all_gather | solution.py:85
  121.3 9.3 %convolution_convert_fusion.1 = bf16[4096,128]{1,0:T(8,128)(2,1)} fusion(bf16[2048,4096]{1,0:T(8,128)(2,1)} %fusion, bf16[2048,128]{1,0:T(8,128)(2,1)S(1)} %all_gather.12), kind=kOutput, calls=%fused_computation.6 | convolution fusion | flops 2148007936 | bytes 18350080 | tf_op jit(solution)/shard_map/dot_general | solution.py:83
  130.7 11.4 %convolution_convert_fusion.2 = bf16[2048,128]{1,0:T(8,128)(2,1)} fusion(bf16[2048,4096]{1,0:T(8,128)(2,1)} %fusion, bf16[4096,128]{1,0:T(8,128)(2,1)} %all-gather.5.cloned.1.call-done), kind=kOutput, calls=%fused_computation.7 | convolution fusion | flops 2147745792 | bytes 18350080 | tf_op jit(solution)/shard_map/dot_general | solution.py:78
  142.1 57.0 %reduce-scatter.5.cloned.1.call-done = bf16[256,128]{1,0:T(8,128)(2,1)} async-done(((bf16[4096,128]{1,0:T(8,128)(2,1)}), bf16[256,128]{1,0:T(8,128)(2,1)}) %reduce-scatter.5.cloned.1.call-update) | async-done | bytes 65552 | tf_op jit(solution)/shard_map/reduce_scatter | solution.py:92
  199.1 1.0 fusion.36
  200.1 1.6 fusion.13
  201.8 30.3 %reduce-scatter.9.cloned.1.call-done = bf16[256,128]{1,0:T(8,128)(2,1)} async-done(((bf16[2048,128]{1,0:T(8,128)(2,1)}), bf16[256,128]{1,0:T(8,128)(2,1)}) %reduce-scatter.9.cloned.1.call-update) | async-done | bytes 65552 | tf_op jit(solution)/shard_map/reduce_scatter | solution.py:89
  232.1 1.0 fusion.33
  233.1 1.0 fusion.12
  234.1 13.3 %all_gather.15 = bf16[2048,128]{1,0:T(8,128)(2,1)S(1)} all-gather(bf16[256,128]{1,0:T(8,128)(2,1)S(1)} %fusion.12), channel_id=1, replica_groups=mesh['row'=16,'col'=8] {'col'}, dimensions={0}, use_global_device_ids=true | all-gather | bytes 589824 | tf_op jit(solution)/shard_map/all_gather | solution.py:85
  247.4 9.3 %convolution_convert_fusion = bf16[4096,128]{1,0:T(8,128)(2,1)} fusion(bf16[2048,4096]{1,0:T(8,128)(2,1)} %fusion, bf16[2048,128]{1,0:T(8,128)(2,1)S(1)} %all_gather.15), kind=kOutput, calls=%fused_computation.5 | convolution fusion | flops 2148007936 | bytes 18350080 | tf_op jit(solution)/shard_map/dot_general | solution.py:83
  256.8 19.2 %all-gather.3.cloned.1.call-done = bf16[4096,128]{1,0:T(8,128)(2,1)} async-done(((bf16[256,128]{1,0:T(8,128)(2,1)}), bf16[4096,128]{1,0:T(8,128)(2,1)}) %all-gather.3.cloned.1.call-update) | async-done | bytes 1048592 | tf_op jit(solution)/shard_map/all_gather | solution.py:80
  276.1 11.3 %convolution_convert_fusion.3 = bf16[2048,128]{1,0:T(8,128)(2,1)} fusion(bf16[2048,4096]{1,0:T(8,128)(2,1)} %fusion, bf16[4096,128]{1,0:T(8,128)(2,1)} %all-gather.3.cloned.1.call-done), kind=kOutput, calls=%fused_computation.8 | convolution fusion | flops 2147745792 | bytes 18350080 | tf_op jit(solution)/shard_map/dot_general | solution.py:78
  287.4 63.7 %reduce-scatter.11.cloned.1.call-done = bf16[256,128]{1,0:T(8,128)(2,1)} async-done(((bf16[4096,128]{1,0:T(8,128)(2,1)}), bf16[256,128]{1,0:T(8,128)(2,1)}) %reduce-scatter.11.cloned.1.call-update) | async-done | bytes 65552 | tf_op jit(solution)/shard_map/reduce_scatter | solution.py:92
  351.1 1.0 fusion.27
  352.1 1.6 fusion.10
  353.7 30.2 %reduce-scatter.7.cloned.1.call-done = bf16[256,128]{1,0:T(8,128)(2,1)} async-done(((bf16[2048,128]{1,0:T(8,128)(2,1)}), bf16[256,128]{1,0:T(8,128)(2,1)}) %reduce-scatter.7.cloned.1.call-update) | async-done | bytes 65552 | tf_op jit(solution)/shard_map/reduce_scatter | solution.py:89
  384.0 1.0 fusion.30
  384.9 1.6 fusion.11
  (45 shorter events, 8.5 us)
Async XLA Ops:
  7.2 48.8 %copy-start = (bf16[64,128]{1,0:T(8,128)(2,1)S(1)}, bf16[64,128]{1,0:T(8,128)(2,1)}, u32[]{:S(2)}) copy-start(bf16[64,128]{1,0:T(8,128)(2,1)} %param.16) | copy-start | bytes 49156
  15.2 20.6 %all-to-all-start = ((s32[128,1,24]{2,1,0:T(1,128)}), s32[128,1,24]{2,1,0:T(1,128)S(1)}, u32[]{:S(2)}, u32[]{:S(2)}) async-start(s32[128,1,24]{2,1,0:T(1,128)} %bitcast.4), calls=%async_computation | async-start | bytes 131072 | tf_op jit(solution)/shard_map/all_to_all | solution.py:64
  35.8 19.1 %all-to-all-start.1 = ((bf16[128,2,768]{2,1,0:T(2,128)(2,1)}), bf16[128,2,768]{2,1,0:T(2,128)(2,1)S(1)}, u32[]{:S(2)}, u32[]{:S(2)}) async-start(bf16[128,2,768]{2,1,0:T(2,128)(2,1)} %reshape.189), calls=%async_computation.1 | async-start | bytes 786432 | tf_op jit(solution)/shard_map/all_to_all | solution.py:63
  42.6 88.1 %all-gather.5.cloned.1.call-start = ((), (), s32[]{:S(2)}) async-start(), calls=%async_computation.9 | async-start | bytes 1114112 | tf_op jit(solution)/shard_map/all_gather | solution.py:80
  76.7 122.5 %reduce-scatter.5.cloned.1.call-start = ((), (), s32[]{:S(2)}) async-start(), calls=%async_computation.6 | async-start | bytes 1114112 | tf_op jit(solution)/shard_map/reduce_scatter | solution.py:92
  130.6 68.6 %copy-start.3 = (bf16[2,128,128]{2,1,0:T(8,128)(2,1)S(1)}, bf16[2,128,128]{2,1,0:T(8,128)(2,1)}, u32[]{:S(2)}) copy-start(bf16[2,128,128]{2,1,0:T(8,128)(2,1)} %param.20) | copy-start | bytes 196612
  130.6 69.6 %copy-start.4 = (bf16[2,128,128]{2,1,0:T(8,128)(2,1)S(1)}, bf16[2,128,128]{2,1,0:T(8,128)(2,1)}, u32[]{:S(2)}) copy-start(bf16[2,128,128]{2,1,0:T(8,128)(2,1)} %param.21) | copy-start | bytes 196612
  130.6 101.5 %reduce-scatter.9.cloned.1.call-start = ((), (), s32[]{:S(2)}) async-start(), calls=%async_computation.10 | async-start | bytes 589824 | tf_op jit(solution)/shard_map/reduce_scatter | solution.py:89
  142.1 134.0 %all-gather.3.cloned.1.call-start = ((), (), s32[]{:S(2)}) async-start(), calls=%async_computation.7 | async-start | bytes 1114112 | tf_op jit(solution)/shard_map/all_gather | solution.py:80
  201.8 149.3 %reduce-scatter.11.cloned.1.call-start = ((), (), s32[]{:S(2)}) async-start(), calls=%async_computation.11 | async-start | bytes 1114112 | tf_op jit(solution)/shard_map/reduce_scatter | solution.py:92
  247.4 139.1 %copy-start.1 = (bf16[64,128]{1,0:T(8,128)(2,1)S(1)}, bf16[64,128]{1,0:T(8,128)(2,1)}, u32[]{:S(2)}) copy-start(bf16[64,128]{1,0:T(8,128)(2,1)} %param.16) | copy-start | bytes 49156
  256.8 94.3 %copy-start.2 = (bf16[256,128]{1,0:T(8,128)(2,1)S(1)}, bf16[256,128]{1,0:T(8,128)(2,1)}, u32[]{:S(2)}) copy-start(bf16[256,128]{1,0:T(8,128)(2,1)} %fusion.13) | copy-start | bytes 196612
  256.8 127.2 %reduce-scatter.7.cloned.1.call-start = ((), (), s32[]{:S(2)}) async-start(), calls=%async_computation.8 | async-start | bytes 589824 | tf_op jit(solution)/shard_map/reduce_scatter | solution.py:89
Sparse Core Ops, SparseCore 0:
  76.8 38.4 all-gather.4
  130.7 68.3 reduce-scatter.4
  201.6 30.4 reduce-scatter.8
  234.7 41.3 all-gather.2
  279.1 71.9 reduce-scatter.10
  353.4 30.4 reduce-scatter.6
where the time goes:
time: 394 us; the launch traced here: 393 us
  waiting for transfers between devices  214 us (54%)
  matrix products  52.9 us (13%)
  other arithmetic  47.4 us (12%)
  blocking collectives  26.4 us (7%)
  local copies, waits for them, and re-layouts  19.8 us (5%)
  starting transfers between devices  18.3 us (5%)
  between operations  14.3 us (4%)
    reduce_scatter x2, waiting for transfers between devices, per_device(): lax.psum_scatter(item_part.astype(jnp.bfloat16), 'row', scatter_dimension...  121 us
    reduce_scatter x2, waiting for transfers between devices, per_device(): lax.psum_scatter(user_part.astype(jnp.bfloat16), 'col', scatter_dimension...  60.5 us
    all_gather x2, blocking collectives, per_device(): lax.all_gather(user_rows, 'col', axis=0, tiled=True)  26.4 us
    convert_element_type x1, other arithmetic, dequantize(): return tiled.reshape(row_count, columns).astype(jnp.bfloat16)  26.4 us
    dot_general x2, matrix products, per_device(): jnp.dot(adjacency, lax.all_gather(item_rows, 'row', axis=0, tiled=True),...  22.7 us
    all_gather x2, waiting for transfers between devices, per_device(): lax.all_gather(item_rows, 'row', axis=0, tiled=True)  19.2 us
    dot_general x2, matrix products, per_device(): lax.dot_general(adjacency, lax.all_gather(user_rows, 'col', axis=0, tiled...  18.6 us
    scatter-add x1, other arithmetic, per_device(): jax.ops.segment_sum(chosen.reshape(-1, D), segment, num_segments=node_cou...  17.3 us
  transfers between devices with their start and end apart: 8, of which 7 were waited for; matrix products, arithmetic and copies ran while one was open for 22% of the time, Pallas kernels for 0%

commit v1 on v0

--- a/solution.py
+++ b/solution.py
@@ -2,6 +2,7 @@
 import jax.numpy as jnp
 from jax import lax
 from jax.sharding import PartitionSpec as P
+from jax.lax import all_to_all, psum
 
 D = 128
 RAW_COLS = 64
@@ -77,7 +78,15 @@
     for layer_index in range(LAYERS):
         user_part = jnp.dot(
             adjacency,
-            lax.all_gather(item_rows, "row", axis=0, tiled=True),
+            jnp.concatenate(
+                all_to_all(
+                    jnp.stack([item_rows] * psum(1, axis_name="row")),
+                    axis_name="row",
+                    split_axis=0,
+                    concat_axis=0,
+                ),
+                0,
+            ),
             preferred_element_type=jnp.float32,
         )
         item_part = lax.dot_general(

time: 394 us -> 380 us (0.964)
  waiting for transfers between devices: 214 us -> 193 us
  starting transfers between devices: 18.3 us -> 29.8 us
  matrix products: 52.9 us -> 47 us
    all_gather x2 -> x0, waiting for transfers between devices: 19.2 us -> none  [per_device(): lax.all_gather(item_rows, 'row', axis=0, tiled=True)]
    reduce_scatter x2, waiting for transfers between devices: 121 us -> 136 us  [per_device(): lax.psum_scatter(item_part.astype(jnp.bfloat16), 'row', scatter_dimension...]
    reduce_scatter x2, waiting for transfers between devices: 60.5 us -> 46.6 us  [per_device(): lax.psum_scatter(user_part.astype(jnp.bfloat16), 'col', scatter_dimension...]
    all_to_all x0 -> x2, starting transfers between devices: none -> 8.58 us  [per_device(): all_to_all(jnp.stack([item_rows] * psum(1, axis_name='row')), axis_name='...]
    dot_general x2, matrix products: 22.7 us -> 18 us  [per_device(): jnp.dot(adjacency, jnp.concatenate(all_to_all(jnp.stack([item_rows] * psu...]
  transfers between devices with their start and end apart: 8 -> 8, of which waited for: 7 -> 5; matrix products, arithmetic and copies ran while one was open for 22% -> 20% of each run, Pallas kernels for 0% -> 0%
where the time goes in v1:
time: 380 us; the launch traced here: 379 us
  waiting for transfers between devices  193 us (51%)
  other arithmetic  47.9 us (13%)
  matrix products  47 us (12%)
  starting transfers between devices  29.8 us (8%)
  blocking collectives  26.4 us (7%)
  local copies, waits for them, and re-layouts  20.6 us (5%)
  between operations  14.1 us (4%)
    reduce_scatter x2, waiting for transfers between devices, per_device(): lax.psum_scatter(item_part.astype(jnp.bfloat16), 'row', scatter_dimension...  136 us
    reduce_scatter x2, waiting for transfers between devices, per_device(): lax.psum_scatter(user_part.astype(jnp.bfloat16), 'col', scatter_dimension...  46.6 us
    convert_element_type x1, other arithmetic, dequantize(): return tiled.reshape(row_count, columns).astype(jnp.bfloat16)  26.9 us
    all_gather x2, blocking collectives, per_device(): lax.all_gather(user_rows, 'col', axis=0, tiled=True)  26.4 us
    dot_general x2, matrix products, per_device(): lax.dot_general(adjacency, lax.all_gather(user_rows, 'col', axis=0, tiled...  18.5 us
    dot_general x2, matrix products, per_device(): jnp.dot(adjacency, jnp.concatenate(all_to_all(jnp.stack([item_rows] * psu...  18 us
    scatter-add x1, other arithmetic, per_device(): jax.ops.segment_sum(chosen.reshape(-1, D), segment, num_segments=node_cou...  17.3 us
    all_to_all x1, starting transfers between devices, per_device(): lax.all_to_all(send_codes, ('row', 'col'), split_axis=0, concat_axis=0, t...  11.1 us
  transfers between devices with their start and end apart: 8, of which 5 were waited for; matrix products, arithmetic and copies ran while one was open for 20% of the time, Pallas kernels for 0%

profile of v1, /device:TPU:0, one launch (start us, length us, event | category | flops | bytes accessed | tf_op | source)
XLA Modules:
  0.0 379.2 jit_solution(14158324501765013143)
XLA Ops:
  8.4 1.0 fusion.2
  10.2 4.3 %scatter_custom_fusion = s32[3072]{0:T(1024)S(1)} fusion(s32[1024]{0:T(1024)S(1)} %get-tuple-element.4, s32[1024]{0:T(1024)S(1)} %get-tuple-element.5, s32[]{:T(128)} %constant.40.clone.1), kind=kCustom, calls=%fused_computation.88 | custom fusion | bytes 12292 | tf_op jit(solution)/shard_map/scatter | solution.py:61
  15.2 11.1 %all-to-all-start = ((s32[128,1,24]{2,1,0:T(1,128)}), s32[128,1,24]{2,1,0:T(1,128)S(1)}, u32[]{:S(2)}, u32[]{:S(2)}) async-start(s32[128,1,24]{2,1,0:T(1,128)} %bitcast.4), calls=%async_computation | async-start | bytes 131072 | tf_op jit(solution)/shard_map/all_to_all | solution.py:65
  27.1 4.9 %mul.54 = f32[16,128,32,128]{3,2,1,0:T(8,128)S(1)} broadcast(f32[16,32]{1,0:T(8,128)S(1)} %convert_multiply_fusion.4), dimensions={0,2} | broadcast | bytes 33556480 | tf_op jit(solution)/shard_map/mul | solution.py:22
  32.0 26.9 %fusion = bf16[2048,4096]{1,0:T(8,128)(2,1)} fusion(f32[256,8,32,128]{3,2,1,0:T(8,128)S(1)} %bitcast.61, bf16[2048,4096]{1,0:T(8,128)(2,1)} %param.17), kind=kLoop, calls=%fused_computation.4 | loop fusion | flops 25165824 | bytes 67108864 | tf_op jit(solution)/shard_map/convert_element_type | solution.py:24
  59.1 3.4 scatter_custom_fusion.1
  62.5 1.2 reshape.201
  63.7 9.9 %all-to-all-start.1 = ((bf16[128,2,768]{2,1,0:T(2,128)(2,1)}), bf16[128,2,768]{2,1,0:T(2,128)(2,1)S(1)}, u32[]{:S(2)}, u32[]{:S(2)}) async-start(bf16[128,2,768]{2,1,0:T(2,128)(2,1)} %reshape.201), calls=%async_computation.1 | async-start | bytes 786432 | tf_op jit(solution)/shard_map/all_to_all | solution.py:64
  75.3 10.5 %all-to-all-done.1 = bf16[128,2,768]{2,1,0:T(2,128)(2,1)S(1)} async-done(((bf16[128,2,768]{2,1,0:T(2,128)(2,1)}), bf16[128,2,768]{2,1,0:T(2,128)(2,1)S(1)}, u32[]{:S(2)}, u32[]{:S(2)}) %all-to-all-start.1) | async-done | bytes 393248 | tf_op jit(solution)/shard_map/all_to_all | solution.py:64
  89.1 17.3 %scatter_custom_fusion.2 = f32[513,128]{1,0:T(8,128)S(1)} fusion(s32[3072]{0:T(1024)S(1)} %bitcast.68, f32[3072,128]{1,0:T(8,128)S(1)} %bitcast.63, f32[]{:T(128)} %constant.23.clone.1), kind=kCustom, calls=%fused_computation.43 | custom fusion | flops 393216 | bytes 262660 | tf_op jit(solution)/shard_map/scatter-add | solution.py:73
  106.5 1.2 stack.5
  107.7 3.7 all-to-all-start.3
  111.4 13.1 %all_gather.6 = bf16[2048,128]{1,0:T(8,128)(2,1)S(1)} all-gather(bf16[256,128]{1,0:T(8,128)(2,1)S(1)} %get-tuple-element.2), channel_id=1, replica_groups=mesh['row'=16,'col'=8] {'col'}, dimensions={0}, use_global_device_ids=true | all-gather | bytes 589824 | tf_op jit(solution)/shard_map/all_gather | solution.py:94
  124.5 9.2 %convolution_convert_fusion.1 = bf16[4096,128]{1,0:T(8,128)(2,1)} fusion(bf16[2048,4096]{1,0:T(8,128)(2,1)} %fusion, bf16[2048,128]{1,0:T(8,128)(2,1)S(1)} %all_gather.6), kind=kOutput, calls=%fused_computation.6 | convolution fusion | flops 2148007936 | bytes 18350080 | tf_op jit(solution)/shard_map/dot_general | solution.py:92
  133.9 9.0 %convolution_convert_fusion.2 = bf16[2048,128]{1,0:T(8,128)(2,1)} fusion(bf16[2048,4096]{1,0:T(8,128)(2,1)} %fusion, bf16[4096,128]{1,0:T(8,128)(2,1)S(1)} %bitcast.64), kind=kOutput, calls=%fused_computation.7 | convolution fusion | flops 2147745792 | bytes 18350080 | tf_op jit(solution)/shard_map/dot_general | solution.py:79
  142.9 63.8 %reduce-scatter.5.cloned.1.call-done = bf16[256,128]{1,0:T(8,128)(2,1)} async-done(((bf16[4096,128]{1,0:T(8,128)(2,1)}), bf16[256,128]{1,0:T(8,128)(2,1)}) %reduce-scatter.5.cloned.1.call-update) | async-done | bytes 65552 | tf_op jit(solution)/shard_map/reduce_scatter | solution.py:101
  206.7 1.0 fusion.36
  207.7 1.0 fusion.13
  208.7 1.2 stack.4
  209.9 4.9 %all-to-all-start.2 = ((bf16[16,256,128]{2,1,0:T(8,128)(2,1)}), bf16[16,256,128]{2,1,0:T(8,128)(2,1)S(1)}, u32[]{:S(2)}, u32[]{:S(2)}) async-start(bf16[16,256,128]{2,1,0:T(8,128)(2,1)} %stack.4), calls=%async_computation.3 | async-start | bytes 2097152 | tf_op jit(solution)/shard_map/all_to_all | solution.py:82
  214.9 25.2 %reduce-scatter.9.cloned.1.call-done = bf16[256,128]{1,0:T(8,128)(2,1)} async-done(((bf16[2048,128]{1,0:T(8,128)(2,1)}), bf16[256,128]{1,0:T(8,128)(2,1)}) %reduce-scatter.9.cloned.1.call-update) | async-done | bytes 65552 | tf_op jit(solution)/shard_map/reduce_scatter | solution.py:98
  240.1 1.0 fusion.33
  241.1 1.0 fusion.12
  242.1 13.3 %all_gather.7 = bf16[2048,128]{1,0:T(8,128)(2,1)S(1)} all-gather(bf16[256,128]{1,0:T(8,128)(2,1)S(1)} %fusion.12), channel_id=1, replica_groups=mesh['row'=16,'col'=8] {'col'}, dimensions={0}, use_global_device_ids=true | all-gather | bytes 589824 | tf_op jit(solution)/shard_map/all_gather | solution.py:94
  255.4 9.0 %convolution_convert_fusion.3 = bf16[2048,128]{1,0:T(8,128)(2,1)} fusion(bf16[2048,4096]{1,0:T(8,128)(2,1)} %fusion, bf16[4096,128]{1,0:T(8,128)(2,1)S(1)} %bitcast.65), kind=kOutput, calls=%fused_computation.8 | convolution fusion | flops 2147745792 | bytes 18350080 | tf_op jit(solution)/shard_map/dot_general | solution.py:79
  264.5 9.2 %convolution_convert_fusion = bf16[4096,128]{1,0:T(8,128)(2,1)} fusion(bf16[2048,4096]{1,0:T(8,128)(2,1)} %fusion, bf16[2048,128]{1,0:T(8,128)(2,1)S(1)} %all_gather.7), kind=kOutput, calls=%fused_computation.5 | convolution fusion | flops 2148007936 | bytes 18350080 | tf_op jit(solution)/shard_map/dot_general | solution.py:92
  273.8 21.4 %reduce-scatter.7.cloned.1.call-done = bf16[256,128]{1,0:T(8,128)(2,1)} async-done(((bf16[2048,128]{1,0:T(8,128)(2,1)}), bf16[256,128]{1,0:T(8,128)(2,1)}) %reduce-scatter.7.cloned.1.call-update) | async-done | bytes 65552 | tf_op jit(solution)/shard_map/reduce_scatter | solution.py:98
  295.2 1.0 fusion.30
  296.2 1.6 fusion.11
  297.8 72.3 %reduce-scatter.11.cloned.1.call-done = bf16[256,128]{1,0:T(8,128)(2,1)} async-done(((bf16[4096,128]{1,0:T(8,128)(2,1)}), bf16[256,128]{1,0:T(8,128)(2,1)}) %reduce-scatter.11.cloned.1.call-update) | async-done | bytes 65552 | tf_op jit(solution)/shard_map/reduce_scatter | solution.py:101
  370.1 1.0 fusion.27
  371.1 1.6 fusion.10
  (47 shorter events, 8.7 us)
Async XLA Ops:
  7.2 79.6 %copy-start = (bf16[64,128]{1,0:T(8,128)(2,1)S(1)}, bf16[64,128]{1,0:T(8,128)(2,1)}, u32[]{:S(2)}) copy-start(bf16[64,128]{1,0:T(8,128)(2,1)} %param.16) | copy-start | bytes 49156
  15.2 48.5 %all-to-all-start = ((s32[128,1,24]{2,1,0:T(1,128)}), s32[128,1,24]{2,1,0:T(1,128)S(1)}, u32[]{:S(2)}, u32[]{:S(2)}) async-start(s32[128,1,24]{2,1,0:T(1,128)} %bitcast.4), calls=%async_computation | async-start | bytes 131072 | tf_op jit(solution)/shard_map/all_to_all | solution.py:65
  32.0 27.0 %copy-start.4 = (bf16[1024,64]{0,1:T(8,128)(2,1)S(1)}, bf16[1024,64]{0,1:T(8,128)(2,1)}, u32[]{:S(2)}) copy-start(bf16[1024,64]{0,1:T(8,128)(2,1)} %param.11) | copy-start | bytes 393220
  32.0 55.3 %copy-start.5 = (bf16[32,128]{1,0:T(8,128)(2,1)S(1)}, bf16[32,128]{1,0:T(8,128)(2,1)}, u32[]{:S(2)}) copy-start(bf16[32,128]{1,0:T(8,128)(2,1)} %param.15) | copy-start | bytes 24580
  63.7 22.1 %all-to-all-start.1 = ((bf16[128,2,768]{2,1,0:T(2,128)(2,1)}), bf16[128,2,768]{2,1,0:T(2,128)(2,1)S(1)}, u32[]{:S(2)}, u32[]{:S(2)}) async-start(bf16[128,2,768]{2,1,0:T(2,128)(2,1)} %reshape.201), calls=%async_computation.1 | async-start | bytes 786432 | tf_op jit(solution)/shard_map/all_to_all | solution.py:64
  107.7 26.1 %all-to-all-start.3 = ((bf16[16,256,128]{2,1,0:T(8,128)(2,1)}), bf16[16,256,128]{2,1,0:T(8,128)(2,1)S(1)}, u32[]{:S(2)}, u32[]{:S(2)}) async-start(bf16[16,256,128]{2,1,0:T(8,128)(2,1)} %stack.5), calls=%async_computation.5 | async-start | bytes 2097152 | tf_op jit(solution)/shard_map/all_to_all | solution.py:82
  111.4 95.3 %reduce-scatter.5.cloned.1.call-start = ((), (), s32[]{:S(2)}) async-start(), calls=%async_computation.8 | async-start | bytes 1114112 | tf_op jit(solution)/shard_map/reduce_scatter | solution.py:101
  133.8 72.9 %copy-start.2 = (bf16[2,128,128]{2,1,0:T(8,128)(2,1)S(1)}, bf16[2,128,128]{2,1,0:T(8,128)(2,1)}, u32[]{:S(2)}) copy-start(bf16[2,128,128]{2,1,0:T(8,128)(2,1)} %param.20) | copy-start | bytes 196612
  133.8 73.9 %copy-start.3 = (bf16[2,128,128]{2,1,0:T(8,128)(2,1)S(1)}, bf16[2,128,128]{2,1,0:T(8,128)(2,1)}, u32[]{:S(2)}) copy-start(bf16[2,128,128]{2,1,0:T(8,128)(2,1)} %param.21) | copy-start | bytes 196612
  133.8 106.3 %reduce-scatter.9.cloned.1.call-start = ((), (), s32[]{:S(2)}) async-start(), calls=%async_computation.10 | async-start | bytes 589824 | tf_op jit(solution)/shard_map/reduce_scatter | solution.py:98
  209.9 45.5 %all-to-all-start.2 = ((bf16[16,256,128]{2,1,0:T(8,128)(2,1)}), bf16[16,256,128]{2,1,0:T(8,128)(2,1)S(1)}, u32[]{:S(2)}, u32[]{:S(2)}) async-start(bf16[16,256,128]{2,1,0:T(8,128)(2,1)} %stack.4), calls=%async_computation.3 | async-start | bytes 2097152 | tf_op jit(solution)/shard_map/all_to_all | solution.py:82
  214.8 80.3 %reduce-scatter.7.cloned.1.call-start = ((), (), s32[]{:S(2)}) async-start(), calls=%async_computation.9 | async-start | bytes 589824 | tf_op jit(solution)/shard_map/reduce_scatter | solution.py:98
  255.4 117.3 %copy-start.1 = (bf16[64,128]{1,0:T(8,128)(2,1)S(1)}, bf16[64,128]{1,0:T(8,128)(2,1)}, u32[]{:S(2)}) copy-start(bf16[64,128]{1,0:T(8,128)(2,1)} %param.16) | copy-start | bytes 49156
  264.5 105.6 %reduce-scatter.11.cloned.1.call-start = ((), (), s32[]{:S(2)}) async-start(), calls=%async_computation.11 | async-start | bytes 1114112 | tf_op jit(solution)/shard_map/reduce_scatter | solution.py:101
Sparse Core Ops, SparseCore 0:
  133.9 72.7 reduce-scatter.4
  209.2 30.8 reduce-scatter.8
  264.6 30.5 reduce-scatter.6
  298.5 71.4 reduce-scatter.10
